TPU v7x, 256 devices: a whole 4x4x8 slice. The times are simulated.
256 devices in a mesh: gx: 64 (over z, x, core), gy: 4 (over y).
Axes of the slice: x: 4, y: 4, z: 8, core: 2. Of those that a mesh axis runs over, the one named last changes fastest.
Arguments:
- conserved: float32 [5, 1024, 64, 512], P(None, 'gx', 'gy'), as said below
- shock_flags: int32 [64, 4, 32], P('gx', 'gy'), may hold values from 0 to 1, as said below
Outputs:
- advanced: float32 [5, 1024, 64, 512], P(None, 'gx', 'gy')
- tendency: float32 [5, 1024, 64, 512], P(None, 'gx', 'gy')
Inputs may be any that keep to these rules, and one draw needn't show every extreme that they name: `shock_flags`: for every block index along the second dimension, the blocks flagged 1 lie within a quarter of the 64 block columns along the first dimension, consecutive when counted cyclically. `conserved`: density and pressure are positive in every cell.
All inputs are finite; a program needn't handle non-finite values.
Results may differ from a plain program's by a relative error of at most 0.0003.
Values sent between devices are 32-bit elements; how exact they have to be, the bound alone decides.
No kernel may reach another device: no remote copies, remote signals or barrier semaphores. Data moves between devices by JAX's collectives and lax.ppermute only.
A program may use at most 128 MiB of HBM per device.

v0:
```python
import jax
import jax.numpy as jnp
from jax import lax
from jax.sharding import PartitionSpec as P

GAMMA = 1.4
GAMMA_LESS = 0.4
COURANT = 0.4
EPSILON = 1e-06


def extended(shard, sides, width):
    for axis, dim in sides:
        size, length = (lax.axis_size(axis), shard.shape[dim])
        up = [(i, (i + 1) % size) for i in range(size)]
        down = [(j, i) for i, j in up]
        last = lax.slice_in_dim(shard, length - width, length, axis=dim)
        first = lax.slice_in_dim(shard, 0, width, axis=dim)
        before = lax.ppermute(last, axis, up)
        after = lax.ppermute(first, axis, down)
        shard = jnp.concatenate([before, shard, after], axis=dim)
    return shard


def shifted(block, axis, distance):
    devices = range(lax.axis_size(axis))
    route = [((i - distance) % len(devices), i) for i in devices]
    return lax.ppermute(block, axis, route)


def pressure_of(density, mom_one, mom_two, mom_three, energy):
    return GAMMA_LESS * (
        energy - 0.5 * (mom_one * mom_one + mom_two * mom_two + mom_three * mom_three) / density
    )


def speed_max(fields):
    density = fields[0]
    pressure = pressure_of(density, fields[1], fields[2], fields[3], fields[4])
    sound_speed = jnp.sqrt(GAMMA * pressure / density)
    speed_sum = (
        jnp.abs(fields[1] / density)
        + sound_speed
        + (jnp.abs(fields[2] / density) + sound_speed)
        + (jnp.abs(fields[3] / density) + sound_speed)
    )
    return jnp.max(speed_sum)


def cell_flux(density, momenta, energy, normal):
    pressure = pressure_of(density, momenta[0], momenta[1], momenta[2], energy)
    velocity = momenta[normal] / density
    fluxes = [momenta[normal]]
    for other in range(3):
        if other == normal:
            fluxes.append(momenta[other] * velocity + pressure)
        else:
            fluxes.append(momenta[other] * velocity)
    fluxes.append((energy + pressure) * velocity)
    return (fluxes, pressure, velocity)


def central_line(fields, normal):
    density = fields[0]
    fluxes, pressure, velocity = cell_flux(
        density, [fields[1], fields[2], fields[3]], fields[4], normal
    )
    faces_count = density.shape[normal] - 5

    def offset(values, shift_by):
        return lax.slice_in_dim(values, shift_by, shift_by + faces_count, axis=normal)

    result = []
    for values in fluxes:
        face_flux = (
            offset(values, 0)
            + offset(values, 5)
            - 8.0 * (offset(values, 1) + offset(values, 4))
            + 37.0 * (offset(values, 2) + offset(values, 3))
        ) / 60.0
        result.append(
            lax.slice_in_dim(face_flux, 1, faces_count, axis=normal)
            - lax.slice_in_dim(face_flux, 0, faces_count - 1, axis=normal)
        )
    return jnp.stack(result)


def central_div(padded):
    size_one = padded.shape[1] - 6
    size_two = padded.shape[2] - 6
    size_three = padded.shape[3] - 6
    along_one = padded[:, :, 3 : 3 + size_two, 3 : 3 + size_three]
    along_two = padded[:, 3 : 3 + size_one, :, 3 : 3 + size_three]
    along_three = padded[:, 3 : 3 + size_one, 3 : 3 + size_two, :]
    return central_line(along_one, 0) + central_line(along_two, 1) + central_line(along_three, 2)


def weno_five(far_left, near_left, centre, near_right, far_right):
    first_guess = (2.0 * far_left - 7.0 * near_left + 11.0 * centre) / 6.0
    second_guess = (-near_left + 5.0 * centre + 2.0 * near_right) / 6.0
    third_guess = (2.0 * centre + 5.0 * near_right - far_right) / 6.0
    smooth_one = (
        13.0 / 12.0 * (far_left - 2.0 * near_left + centre) ** 2
        + 0.25 * (far_left - 4.0 * near_left + 3.0 * centre) ** 2
    )
    smooth_two = (
        13.0 / 12.0 * (near_left - 2.0 * centre + near_right) ** 2
        + 0.25 * (near_left - near_right) ** 2
    )
    smooth_three = (
        13.0 / 12.0 * (centre - 2.0 * near_right + far_right) ** 2
        + 0.25 * (3.0 * centre - 4.0 * near_right + far_right) ** 2
    )
    weight_one = 0.1 / (EPSILON + smooth_one) ** 2
    weight_two = 0.6 / (EPSILON + smooth_two) ** 2
    weight_three = 0.3 / (EPSILON + smooth_three) ** 2
    return (weight_one * first_guess + weight_two * second_guess + weight_three * third_guess) / (
        weight_one + weight_two + weight_three
    )


def weno_axis(lines, axis):
    faces_count = lines[0].shape[axis] - 5
    density = lines[0]
    fluxes, pressure, velocity = cell_flux(density, [lines[1], lines[2], lines[3]], lines[4], 0)
    sound_speed = jnp.sqrt(GAMMA * pressure / density)
    enthalpy = (lines[4] + pressure) / density
    vel_two = lines[2] / density
    vel_three = lines[3] / density

    def offset(values, shift_by):
        return lax.slice_in_dim(values, shift_by, shift_by + faces_count, axis=axis)

    wave_speed = jnp.abs(velocity) + sound_speed
    alpha_face = offset(wave_speed, 0)
    for shift_by in range(1, 6):
        alpha_face = jnp.maximum(alpha_face, offset(wave_speed, shift_by))
    mean_one = 0.5 * (offset(velocity, 2) + offset(velocity, 3))
    mean_two = 0.5 * (offset(vel_two, 2) + offset(vel_two, 3))
    mean_three = 0.5 * (offset(vel_three, 2) + offset(vel_three, 3))
    mean_enth = 0.5 * (offset(enthalpy, 2) + offset(enthalpy, 3))
    kinetic = 0.5 * (mean_one * mean_one + mean_two * mean_two + mean_three * mean_three)
    sound_sq = GAMMA_LESS * (mean_enth - kinetic)
    mean_sound = jnp.sqrt(sound_sq)
    inv_sound = 1.0 / mean_sound
    coef_one = GAMMA_LESS / sound_sq
    coef_two = coef_one * kinetic
    left_first = [
        0.5 * (coef_two + mean_one * inv_sound),
        -0.5 * (coef_one * mean_one + inv_sound),
        -0.5 * coef_one * mean_two,
        -0.5 * coef_one * mean_three,
        0.5 * coef_one,
    ]
    left_second = [
        1.0 - coef_two,
        coef_one * mean_one,
        coef_one * mean_two,
        coef_one * mean_three,
        -coef_one,
    ]
    left_last = [
        0.5 * (coef_two - mean_one * inv_sound),
        -0.5 * (coef_one * mean_one - inv_sound),
        -0.5 * coef_one * mean_two,
        -0.5 * coef_one * mean_three,
        0.5 * coef_one,
    ]

    def project(split_flux):
        waves = []
        waves.append(
            left_first[0] * split_flux[0]
            + left_first[1] * split_flux[1]
            + left_first[2] * split_flux[2]
            + left_first[3] * split_flux[3]
            + left_first[4] * split_flux[4]
        )
        waves.append(
            left_second[0] * split_flux[0]
            + left_second[1] * split_flux[1]
            + left_second[2] * split_flux[2]
            + left_second[3] * split_flux[3]
            + left_second[4] * split_flux[4]
        )
        waves.append(split_flux[2] - mean_two * split_flux[0])
        waves.append(split_flux[3] - mean_three * split_flux[0])
        waves.append(
            left_last[0] * split_flux[0]
            + left_last[1] * split_flux[1]
            + left_last[2] * split_flux[2]
            + left_last[3] * split_flux[3]
            + left_last[4] * split_flux[4]
        )
        return waves

    plus_waves = []
    minus_waves = []
    for shift_by in range(6):
        state_part = [offset(lines[component], shift_by) for component in range(5)]
        flux_part = [offset(fluxes[component], shift_by) for component in range(5)]
        plus_waves.append(
            project(
                [
                    0.5 * (flux_part[component] + alpha_face * state_part[component])
                    for component in range(5)
                ]
            )
        )
        minus_waves.append(
            project(
                [
                    0.5 * (flux_part[component] - alpha_face * state_part[component])
                    for component in range(5)
                ]
            )
        )
    totals = []
    for channel in range(5):
        upwind = weno_five(
            plus_waves[0][channel],
            plus_waves[1][channel],
            plus_waves[2][channel],
            plus_waves[3][channel],
            plus_waves[4][channel],
        )
        downwind = weno_five(
            minus_waves[5][channel],
            minus_waves[4][channel],
            minus_waves[3][channel],
            minus_waves[2][channel],
            minus_waves[1][channel],
        )
        totals.append(upwind + downwind)
    shared = totals[0] + totals[1] + totals[4]
    faces = [
        shared,
        (mean_one - mean_sound) * totals[0]
        + mean_one * totals[1]
        + (mean_one + mean_sound) * totals[4],
        mean_two * shared + totals[2],
        mean_three * shared + totals[3],
        (mean_enth - mean_one * mean_sound) * totals[0]
        + kinetic * totals[1]
        + mean_two * totals[2]
        + mean_three * totals[3]
        + (mean_enth + mean_one * mean_sound) * totals[4],
    ]
    return faces


def slab_weno(slab_fields):
    edge_cells = slab_fields.shape[1] - 6
    slab_cells = slab_fields.shape[3] - 6
    views = (
        (0, slab_fields[:, :, 3 : 3 + edge_cells, 3 : 3 + slab_cells]),
        (1, slab_fields[:, 3 : 3 + edge_cells, :, 3 : 3 + slab_cells]),
        (2, slab_fields[:, 3 : 3 + edge_cells, 3 : 3 + edge_cells, :]),
    )
    total_div = None
    for normal, view in views:
        order = [0, 1 + normal] + [1 + other for other in range(3) if other != normal] + [4]
        faces = weno_axis([view[component] for component in order], normal)
        faces_count = faces[0].shape[normal]
        restored = [None] * 5
        for position, component in enumerate(order):
            restored[component] = lax.slice_in_dim(
                faces[position], 1, faces_count, axis=normal
            ) - lax.slice_in_dim(faces[position], 0, faces_count - 1, axis=normal)
        div_part = jnp.stack(restored)
        total_div = div_part if total_div is None else total_div + div_part
    return total_div


def slab_empty(slab_fields):
    edge_cells = slab_fields.shape[1] - 6
    slab_cells = slab_fields.shape[3] - 6
    return jnp.zeros((5, edge_cells, edge_cells, slab_cells), jnp.float32)


def group_div(slab_fields, chosen):
    return lax.cond(jnp.any(chosen > 0), slab_weno, slab_empty, slab_fields)


def spread_groups(padded, column_flags, portions, lend_out, lend_back):
    edge_cells = padded.shape[1] - 6
    group_size = column_flags.shape[2] // portions
    slab_cells = group_size * edge_cells
    axis_size = lax.axis_size("gx")
    position = lax.axis_index("gx")
    stride = axis_size // portions
    results = []
    for portion in range(portions):
        slab_fields = padded[:, :, :, portion * slab_cells : portion * slab_cells + slab_cells + 6]
        if portion == 0:
            arrived = slab_fields
            source = position
        else:
            arrived = lend_out(
                slab_fields.reshape(5, edge_cells + 6, -1), portion * stride
            ).reshape(slab_fields.shape)
            source = (position - portion * stride) % axis_size
        source_flags = lax.dynamic_index_in_dim(column_flags, source, 0, keepdims=False)[0]
        chosen = source_flags[portion * group_size : (portion + 1) * group_size]
        slab_div = group_div(arrived, chosen)
        if portion > 0:
            slab_div = lend_back(
                slab_div.reshape(5, edge_cells, -1), axis_size - portion * stride
            ).reshape(slab_div.shape)
        results.append(slab_div)
    return jnp.concatenate(results, axis=3)


def shards(conserved, shock_flags):
    edge_cells = conserved.shape[1]
    padded = extended(conserved, (("gx", 1), ("gy", 2)), 3)
    padded = jnp.concatenate([padded[:, :, :, -3:], padded, padded[:, :, :, :3]], axis=3)
    global_speed = lax.pmax(speed_max(conserved), ("gx", "gy"))
    step_size = COURANT / global_speed
    central = central_div(padded)
    column_flags = lax.all_gather(shock_flags, "gx", axis=0, tiled=True)

    def lend_out(payload, distance):
        return shifted(payload, "gx", distance)

    def lend_back(payload, distance):
        return shifted(payload, "gx", distance)

    weno_part = spread_groups(padded, column_flags, 2, lend_out, lend_back)
    shock_cells = jnp.repeat(shock_flags[0, 0], edge_cells) > 0
    divergence = jnp.where(shock_cells, weno_part, central)
    tendency = -divergence
    advanced = conserved + step_size * tendency
    return (advanced, tendency)


def solution(mesh):
    return jax.shard_map(
        shards,
        mesh=mesh,
        in_specs=(P(None, "gx", "gy", None), P("gx", "gy", None)),
        out_specs=(P(None, "gx", "gy", None), P(None, "gx", "gy", None)),
        check_vma=False,
    )
```

profile of v0, /device:TPU:8, one launch (start us, length us, event | category | flops | bytes accessed | tf_op | source)
XLA Modules:
  0.0 521.7 jit_solution(2541666270935029508)
XLA Ops:
  0.6 2.4 fusion.544
  3.0 7.5 %collective-permute-start.1 = (f32[5,3,16,512]{3,2,1,0:T(8,128)}, f32[5,3,16,512]{3,2,1,0:T(8,128)S(1)}, u32[]{:S(2)}, u32[]{:S(2)}) collective-permute-start(f32[5,3,16,512]{3,2,1,0:T(8,128)} %get-tuple-element.670), channel_id=1, source_target_pairs={{4,0},{8,4},{12,8},{16,12},{20,16},{24,20},{28,24},{32,28},{36,32}... | collective-permute-start | bytes 1474568 | tf_op jit(solution)/shard_map/ppermute | solution.py:20
  10.5 40.4 %all_gather.3 = s32[64,1,32]{2,1,0:T(1,128)S(1)} all-gather(s32[1,1,32]{2,1,0:T(1,128)} %param.7), channel_id=1, replica_groups=mesh['gx'=64,'gy'=4] {'gx'}, dimensions={0}, use_global_device_ids=true | all-gather | bytes 8320 | tf_op jit(solution)/shard_map/all_gather | solution.py:321
  52.3 2.9 fusion.499
  55.8 74.0 %pmax.7 = f32[]{:T(128)} all-reduce(f32[]{:T(128)} %fusion.499), channel_id=1, replica_groups=mesh['gx'=64,'gy'=4] {'gx','gy'}, use_global_device_ids=true, to_apply=%region_1.0 | all-reduce | flops 1 | bytes 8 | tf_op jit(solution)/shard_map/pmax | solution.py:318
  136.7 1.5 collective-permute-start.2
  139.7 14.4 %collective-permute-done.3 = f32[5,22,3,512]{3,1,2,0:T(8,128)S(1)} collective-permute-done((f32[5,22,3,512]{3,1,2,0:T(8,128)S(1)}, f32[5,22,3,512]{3,1,2,0:T(8,128)S(1)}, u32[]{:S(2)}, u32[]{:S(2)}) %collective-permute-start.3) | collective-permute-done | bytes 675872 | tf_op jit(solution)/shard_map/ppermute | solution.py:20
  158.0 1.8 copy-done.3
  159.8 4.6 pad_maximum_fusion.1
  164.4 1.6 add_multiply_fusion.120
  170.5 5.1 reshape.107
  175.6 2.4 collective-permute-start.4
  178.1 1.8 fusion.411
  183.8 1.4 add_multiply_fusion.118
  188.3 6.1 %maximum_maximum_fusion = f32[5,22,22,515]{3,2,1,0:T(8,128)} fusion(f32[5,22,3,512]{3,2,1,0:T(4,128)S(1)} %copy.72, f32[5,22,16,512]{3,2,1,0:T(8,128)S(1)} %copy-done.1, f32[5,22,3,512]{3,2,1,0:T(4,128)S(1)} %copy-done.8, f32[5,22,22,3]{3,2,1,0:T(8,128)S(1)} %copy-done.10), kind=kLoop, calls=%fused_computation.1032 | loop fusion | flops 3738900 | bytes 9970400 | tf_op jit(solution)/shard_map/concatenate | solution.py:317
  194.4 2.1 fusion.380
  196.5 106.8 %collective-permute-done.4 = f32[5,22,5764]{2,1,0:T(8,128)} collective-permute-done((f32[5,22,5764]{2,1,0:T(8,128)}, f32[5,22,5764]{2,1,0:T(8,128)}, u32[]{:S(2)}, u32[]{:S(2)}) %collective-permute-start.4) | collective-permute-done | bytes 2536192 | tf_op jit(solution)/shard_map/ppermute | solution.py:28
  303.2 7.5 %conditional.3 = (f32[5,16,16,256]{3,1,2,0:T(8,128)S(1)}) conditional(s32[]{:T(128)} %convert_element_type.7, () %tuple.21, f32[5,22,5764]{2,1,0:T(8,128)} %collective-permute-done.4), branch_computations={%region_6.7_spmd, %region_7.8_spmd} | conditional | flops 240528128 | bytes 275007200 | solution.py:282
  312.0 92.7 %collective-permute-start.5 = (f32[5,16,4096]{2,1,0:T(8,128)}, f32[5,16,4096]{2,1,0:T(8,128)}, u32[]{:S(2)}, u32[]{:S(2)}) collective-permute-start(f32[5,16,4096]{2,1,0:T(8,128)} %bitcast.156), channel_id=1, source_target_pairs={{128,0},{132,4},{136,8},{140,12},{144,16},{148,20},{152,24},{156,2... | collective-permute-start | bytes 3932168 | tf_op jit(solution)/shard_map/ppermute | solution.py:28
  405.6 105.0 %conditional.2 = (f32[5,16,16,256]{3,2,1,0:T(8,128)S(1)}) conditional(s32[]{:T(128)} %convert_element_type.6, () %tuple.20, f32[5,22,22,515]{3,2,1,0:T(8,128)} %maximum_maximum_fusion), branch_computations={%region_3.4_spmd, %region_4.5_spmd} | conditional | flops 240528128 | bytes 288257600 | solution.py:282
  405.6 2.1 fusion.536
  417.0 36.0 %multiply_add_fusion = (f32[16,16,257]{2,0,1:T(8,128)S(1)}, f32[16,16,257]{2,0,1:T(8,128)S(1)}, f32[16,16,257]{2,0,1:T(8,128)S(1)}, f32[16,16,257]{2,0,1:T(8,128...) fusion(f32[16,16,257]{2,0,1:T(8,128)S(1)} %get-tuple-element.23, ...), kind=kLoop, calls=%fused_computation.177 | loop fusion | flops 64081408 | bytes 17895424 | tf_op jit(solution)/shard_map/cond/branch_1_fun/add | solution.py:243
  457.9 13.2 %multiply_add_fusion.13 = (f32[16,17,256]{2,0,1:T(8,128)S(1)}, f32[16,17,256]{2,0,1:T(8,128)S(1)}, f32[16,17,256]{2,0,1:T(8,128)S(1)}, f32[16,17,256]{2,0,1:T(8,...) fusion(f32[16,17,256]{2,0,1:T(8,128)S(1)} %get-tuple-element.31, ...), kind=kLoop, calls=%fused_computation.363 | loop fusion | flops 67821568 | bytes 18939904 | tf_op jit(solution)/shard_map/cond/branch_1_fun/add | solution.py:243
  474.9 2.0 fusion.534
  477.3 3.4 fusion.533
  480.6 2.3 fusion.27
  484.5 1.8 fusion.28
  486.4 2.1 fusion.26
  488.5 1.9 fusion.29
  490.4 18.2 %multiply_add_fusion.5 = (f32[17,16,256]{2,0,1:T(8,128)S(1)}, f32[17,16,256]{2,0,1:T(8,128)S(1)}, f32[17,16,256]{2,0,1:T(8,128)S(1)}, f32[17,16,256]{2,0,1:T(8,1...) fusion(f32[17,16,256]{2,0,1:T(8,128)S(1)} %get-tuple-element.36, ...), kind=kLoop, calls=%fused_computation.232 | loop fusion | flops 67821568 | bytes 18939904 | tf_op jit(solution)/shard_map/cond/branch_1_fun/add | solution.py:243
  515.3 1.9 copy.169
  517.6 3.8 multiply_add_fusion.34
  (185 shorter events, 52.1 us)
Async XLA Ops:
  0.6 133.0 %copy-start.5 = (f32[5,16,16,512]{3,2,1,0:T(8,128)S(1)}, f32[5,16,16,512]{3,2,1,0:T(8,128)}, u32[]{:S(2)}) copy-start(f32[5,16,16,512]{3,2,1,0:T(8,128)} %param.6) | copy-start | bytes 7864324
  3.0 129.4 %collective-permute-start = (f32[5,3,16,512]{3,2,1,0:T(8,128)}, f32[5,3,16,512]{3,2,1,0:T(8,128)}, u32[]{:S(2)}, u32[]{:S(2)}) collective-permute-start(f32[5,3,16,512]{3,2,1,0:T(8,128)} %get-tuple-element.671), channel_id=1, source_target_pairs={{0,4},{4,8},{8,12},{12,16},{16,20},{20,24},{24,28},{28,32},{32,36}... | collective-permute-start | bytes 1474568 | tf_op jit(solution)/shard_map/ppermute | solution.py:19
  3.0 131.4 %collective-permute-start.1 = (f32[5,3,16,512]{3,2,1,0:T(8,128)}, f32[5,3,16,512]{3,2,1,0:T(8,128)S(1)}, u32[]{:S(2)}, u32[]{:S(2)}) collective-permute-start(f32[5,3,16,512]{3,2,1,0:T(8,128)} %get-tuple-element.670), channel_id=1, source_target_pairs={{4,0},{8,4},{12,8},{16,12},{20,16},{24,20},{28,24},{32,28},{36,32}... | collective-permute-start | bytes 1474568 | tf_op jit(solution)/shard_map/ppermute | solution.py:20
  134.5 29.9 %copy-start = (f32[5,22,16,512]{3,2,1,0:T(8,128)}, f32[5,22,16,512]{3,2,1,0:T(8,128)S(1)}, u32[]{:S(2)}) copy-start(f32[5,22,16,512]{3,2,1,0:T(8,128)S(1)} %get-tuple-element.678) | copy-start | bytes 10813444
  135.7 18.4 %collective-permute-start.3 = (f32[5,22,3,512]{3,1,2,0:T(8,128)S(1)}, f32[5,22,3,512]{3,1,2,0:T(8,128)S(1)}, u32[]{:S(2)}, u32[]{:S(2)}) collective-permute-start(f32[5,22,3,512]{3,1,2,0:T(8,128)S(1)} %copy.70), channel_id=1, source_target_pairs={{1,0},{2,1},{3,2},{0,3},{5,4},{6,5},{7,6},{4,7},{9,8},{10,9},{11,1... | collective-permute-start | bytes 2027528 | tf_op jit(solution)/shard_map/ppermute | solution.py:20
  136.7 19.0 %collective-permute-start.2 = (f32[5,22,3,512]{3,1,2,0:T(8,128)S(1)}, f32[5,22,3,512]{3,1,2,0:T(8,128)S(1)}, u32[]{:S(2)}, u32[]{:S(2)}) collective-permute-start(f32[5,22,3,512]{3,1,2,0:T(8,128)S(1)} %copy.69), channel_id=1, source_target_pairs={{0,1},{1,2},{2,3},{3,0},{4,5},{5,6},{6,7},{7,4},{8,9},{9,10},{10,1... | collective-permute-start | bytes 2027528 | tf_op jit(solution)/shard_map/ppermute | solution.py:19
  139.7 16.0 %copy-start.16 = (f32[5,16,16,512]{3,2,1,0:T(8,128)}, f32[5,16,16,512]{3,2,1,0:T(8,128)S(1)}, u32[]{:S(2)}) copy-start(f32[5,16,16,512]{3,2,1,0:T(8,128)S(1)} %fusion.476) | copy-start | bytes 7864324
  156.2 8.2 %copy-start.7 = (f32[5,22,3,512]{3,2,1,0:T(4,128)}, f32[5,22,3,512]{3,2,1,0:T(4,128)S(1)}, u32[]{:S(2)}) copy-start(f32[5,22,3,512]{3,2,1,0:T(4,128)S(1)} %copy.71) | copy-start | bytes 2027524
  157.4 2.3 copy-start.3
  159.8 4.6 copy-start.9
  175.6 127.6 %collective-permute-start.4 = (f32[5,22,5764]{2,1,0:T(8,128)}, f32[5,22,5764]{2,1,0:T(8,128)}, u32[]{:S(2)}, u32[]{:S(2)}) collective-permute-start(f32[5,22,5764]{2,1,0:T(8,128)} %reshape.107), channel_id=1, source_target_pairs={{128,0},{132,4},{136,8},{140,12},{144,16},{148,20},{152,24},{156,2... | collective-permute-start | bytes 7608488 | tf_op jit(solution)/shard_map/ppermute | solution.py:28
  178.1 5.7 %slice-start.2 = ((s8[5406720]{0:T(1024)(128)(4,1)}), s8[1212416]{0:T(1024)(128)(4,1)S(1)}, s32[]{:S(2)}) async-start(s8[5406720]{0:T(1024)(128)(4,1)} %bitcast.1120), calls=%async_computation.2 | async-start | bytes 2424832
  179.8 3.9 slice-start.3
  185.7 2.4 copy-start.1
  185.7 2.6 copy-start.8
  312.0 203.4 %collective-permute-start.5 = (f32[5,16,4096]{2,1,0:T(8,128)}, f32[5,16,4096]{2,1,0:T(8,128)}, u32[]{:S(2)}, u32[]{:S(2)}) collective-permute-start(f32[5,16,4096]{2,1,0:T(8,128)} %bitcast.156), channel_id=1, source_target_pairs={{128,0},{132,4},{136,8},{140,12},{144,16},{148,20},{152,24},{156,2... | collective-permute-start | bytes 3932168 | tf_op jit(solution)/shard_map/ppermute | solution.py:28
  405.6 105.1 %copy-start.11 = (f32[16,17,512]{2,1,0:T(8,128)S(1)}, f32[16,17,512]{2,1,0:T(8,128)}, u32[]{:S(2)}) copy-start(f32[16,17,512]{2,1,0:T(8,128)} %fusion.390) | copy-start | bytes 1671172
  405.6 106.0 %copy-start.13 = (f32[16,17,512]{2,1,0:T(8,128)S(1)}, f32[16,17,512]{2,1,0:T(8,128)}, u32[]{:S(2)}) copy-start(f32[16,17,512]{2,1,0:T(8,128)} %get-tuple-element.686) | copy-start | bytes 1671172
  415.9 38.3 %slice-start = ((s8[6758400]{0:T(1024)(128)(4,1)}), s8[4194304]{0:T(1024)(128)(4,1)S(1)}, s32[]{:S(2)}) async-start(s8[6758400]{0:T(1024)(128)(4,1)} %bitcast.1118), calls=%async_computation | async-start | bytes 8388608 | tf_op jit(solution)/shard_map/cond
  417.0 37.2 %slice-start.1 = ((s8[6758400]{0:T(1024)(128)(4,1)}), s8[2564096]{0:T(1024)(128)(4,1)S(1)}, s32[]{:S(2)}) async-start(s8[6758400]{0:T(1024)(128)(4,1)} %bitcast.1118), calls=%async_computation.1 | async-start | bytes 5128192 | tf_op jit(solution)/shard_map/cond
  480.6 2.4 copy-start.45
  480.6 2.4 copy-start.46
  484.5 1.9 copy-start.28
  484.5 1.9 copy-start.29
  484.5 1.9 copy-start.30
  486.4 2.1 copy-start.18
  486.4 2.1 copy-start.19
  510.7 2.7 copy-start.4
  512.5 4.7 copy-start.17
  513.4 3.8 copy-start.15
  515.2 2.3 copy-start.6
  515.2 2.3 copy-start.47
  (13 other events, 19.3 us)
where the time goes:
time: 528 us; the launch traced here: 522 us
  other arithmetic  137 us (26%)
  waiting for transfers between devices  122 us (23%)
  blocking collectives  114 us (22%)
  starting transfers between devices  105 us (20%)
  local copies, waits for them, and re-layouts  31.3 us (6%)
  loops' own time  8.23 us (2%)
    ppermute x2, waiting for transfers between devices, shifted(): return lax.ppermute(block, axis, route)  107 us
    ppermute x2, starting transfers between devices, shifted(): return lax.ppermute(block, axis, route)  95.1 us
    pmax x1, blocking collectives, shards(): global_speed = lax.pmax(speed_max(conserved), ('gx', 'gy'))  74 us
    add x3, other arithmetic, weno_axis(): (mean_enth - mean_one * mean_sound) * totals[0] + kinetic * totals[1]  67.4 us
    all_gather x1, blocking collectives, shards(): column_flags = lax.all_gather(shock_flags, 'gx', axis=0, tiled=True)  40.4 us
    mul x17, other arithmetic, weno_axis(): 0.5 * (flux_part[component] + alpha_face * state_part[component])  16.8 us
    ppermute x2, waiting for transfers between devices, extended(): after = lax.ppermute(first, axis, down)  14.4 us
    concatenate x2, other arithmetic, shards(): jnp.concatenate([padded[:, :, :, -3:], padded, padded[:, :, :, :3]], axis=3)  10.6 us
  transfers between devices with their start and end apart: 6, of which 3 were waited for; matrix products, arithmetic and copies ran while one was open for 26% of the time, Pallas kernels for 0%

commit v1 on v0

v1 whole, which is shorter than its diff:
```python
import functools

import jax
import jax.numpy as jnp
from jax import lax
from jax.experimental import pallas as pl
from jax.experimental.pallas import tpu as pltpu
from jax.sharding import PartitionSpec as P

GAMMA = 1.4
GAMMA_LESS = 0.4
COURANT = 0.4
EPSILON = 1e-06
LANES = 128
ROWS = 8


def inverse(value):
    guess = pltpu.reciprocal(value, approx=True)
    return guess * (2.0 - value * guess)


def cell_values(density, mom, energy):
    inv = inverse(density)
    inv_half = 0.5 * inv
    half_vel = [m * inv_half for m in mom]
    kinetic = mom[0] * half_vel[0] + mom[1] * half_vel[1] + mom[2] * half_vel[2]
    pressure = GAMMA_LESS * (energy - kinetic)
    total = energy + pressure
    half_enth = total * inv_half
    sound = jnp.sqrt(GAMMA * pressure * inv)
    return half_vel, half_enth, pressure, total, sound


def half_flux(mom, half_vel, pressure, total, normal):
    half_normal = half_vel[normal]
    flux = [0.5 * mom[normal]]
    for other in range(3):
        part = mom[other] * half_normal
        flux.append(part + 0.5 * pressure if other == normal else part)
    flux.append(total * half_normal)
    return flux


def pair_order(normal):
    return [normal] + [other for other in range(3) if other != normal]


def recon_rest(d1, d2, d3, d4):
    t1 = d2 - d1
    t2 = d3 - d2
    t3 = d4 - d3
    d2s = 0.75 * d2
    d3s = 0.75 * d3
    b0 = t1 * t1 + d2s * (d2 + t1) + 0.75 * EPSILON
    b1 = t2 * t2 + d2s * d3 + 0.75 * EPSILON
    b2 = t3 * t3 + d3s * (d3 - t3) + 0.75 * EPSILON
    r0 = inverse(b0)
    r1 = inverse(b1)
    r2 = inverse(b2)
    z0 = r0 * r0
    z1 = r1 * r1
    z2 = 1.5 * (r2 * r2)
    num = z0 * (t2 - t1) + z2 * (t3 - t2)
    den = z2 + (0.5 * z0 + 3.0 * z1)
    return num * inverse(den)


def central_rest(d_flux):
    return [
        (1.0 / 30.0) * ((d_flux[4][c] - d_flux[0][c]) - 7.0 * (d_flux[3][c] - d_flux[1][c]))
        for c in range(5)
    ]


def weno_rest(d_flux, d_state, mean, alpha, normal):
    order = [0] + [1 + n for n in pair_order(normal)] + [4]
    a, b, e, h = mean
    twice_k = a * a + b * b + e * e
    k = 0.5 * twice_k
    s_sq = GAMMA_LESS * (h - k)
    inv_s = lax.rsqrt(s_sq)
    s = s_sq * inv_s
    half_g = (0.5 * GAMMA_LESS) * (inv_s * inv_s)
    half_inv = 0.5 * inv_s

    def project(x):
        x1 = x[1] - a * x[0]
        x2 = x[2] - b * x[0]
        x3 = x[3] - e * x[0]
        y = half_g * (x[4] - a * x1 - b * x2 - e * x3 - k * x[0])
        z = half_inv * x1
        return [y - z, x[0] - (y + y), x2, x3, y + z]

    up = []
    down = []
    for step in range(5):
        scaled = [alpha * d_state[step][c] for c in order]
        flux = [d_flux[step][c] for c in order]
        up.append([f + q for f, q in zip(flux, scaled)] if step < 4 else None)
        down.append([f - q for f, q in zip(flux, scaled)] if step > 0 else None)
    linear = [(up[1][c] - down[3][c]) - (up[2][c] - down[2][c]) for c in range(5)]
    up = [project(x) if x is not None else None for x in up]
    down = [project(x) if x is not None else None for x in down]
    t = [
        recon_rest(up[0][c], up[1][c], up[2][c], up[3][c])
        - recon_rest(down[4][c], down[3][c], down[2][c], down[1][c])
        for c in range(5)
    ]
    outer = t[0] + t[4]
    shared = outer + t[1]
    swing = s * (t[4] - t[0])
    back = [
        shared,
        a * shared + swing,
        b * shared + t[2],
        e * shared + t[3],
        h * outer + k * t[1] + b * t[2] + e * t[3] + a * swing,
    ]
    rest = [None] * 5
    for position, component in enumerate(order):
        rest[component] = (1.0 / 6.0) * (linear[position] - back[position])
    return rest


def along_lanes(any_ref, q_ref, mask_ref, out_ref, d_ref, s_ref, m_ref, g_ref, x_ref):
    normal = 2
    groups = q_ref.shape[3] // LANES

    def parts(value):
        return [value[:, g * LANES : (g + 1) * LANES] for g in range(groups)]

    def prev(value):
        return pltpu.roll(value, 1, 1)

    def put(ref, index, value):
        for g, part in enumerate(parts(value)):
            ref[(g,) + index] = part

    width = q_ref.shape[3]

    def tile(row, carry):
        rows = pl.ds(pl.multiple_of(row * ROWS, ROWS), ROWS)
        q = [q_ref[c, 0, rows, :] for c in range(5)]
        half_vel, half_enth, pressure, total, sound = cell_values(q[0], q[1:4], q[4])
        flux = half_flux(q[1:4], half_vel, pressure, total, normal)
        wave = jnp.abs(2.0 * half_vel[normal]) + sound
        for position, n in enumerate(pair_order(normal)):
            put(m_ref, (position,), half_vel[n] + prev(half_vel[n]))
        put(m_ref, (3,), half_enth + prev(half_enth))
        two = jnp.maximum(wave, prev(wave))
        alpha = jnp.maximum(jnp.maximum(pltpu.roll(two, 2, 1), two), pltpu.roll(two, width - 2, 1))
        put(m_ref, (4,), alpha)
        for c in range(5):
            before = prev(flux[c])
            put(s_ref, (c,), flux[c] + before)
            diff = flux[c] - before
            half = 0.5 * q[c]
            diff_q = half - prev(half)
            for step, amount in enumerate((2, 1, 0, width - 1, width - 2)):
                put(d_ref, (step, c), pltpu.roll(diff, amount, 1) if amount else diff)
                put(d_ref, (step, 5 + c), pltpu.roll(diff_q, amount, 1) if amount else diff_q)

        def face(g, carry):
            d_flux = [[d_ref[g, k, c] for c in range(5)] for k in range(5)]
            rest = central_rest(d_flux)
            for c in range(5):
                g_ref[g, c] = s_ref[g, c] + rest[c]

            @pl.when(any_ref[g] > 0)
            def _():
                d_flux = [[d_ref[g, k, c] for c in range(5)] for k in range(5)]
                d_state = [[d_ref[g, k, 5 + c] for c in range(5)] for k in range(5)]
                rest = central_rest(d_flux)
                mean = [m_ref[g, n] for n in range(4)]
                weno = weno_rest(d_flux, d_state, mean, m_ref[g, 4], normal)
                for c in range(5):
                    x_ref[g, c] = weno[c] - rest[c]

            @pl.when(any_ref[g] <= 0)
            def _():
                for c in range(5):
                    x_ref[g, c] = jnp.zeros((ROWS, LANES), jnp.float32)

            return carry

        lax.fori_loop(0, groups, face, 0)
        shock = mask_ref[...] > 0.0
        for c in range(5):
            full = jnp.concatenate([g_ref[g, c] for g in range(groups)], axis=1)
            more = jnp.concatenate([x_ref[g, c] for g in range(groups)], axis=1)
            base = full - pltpu.roll(full, width - 1, 1)
            extra = more - pltpu.roll(more, width - 1, 1)
            out_ref[c, 0, rows, :] = base + jnp.where(shock, extra, 0.0)
        return carry

    lax.fori_loop(0, q_ref.shape[2] // ROWS, tile, 0)


def along_others(
    any_ref, step_ref, q_ref, xl_ref, xr_ref, yl_ref, yr_ref, az_ref, mask_ref, adv_ref, ten_ref, p_ref, ty_ref
):
    group = pl.program_id(0)
    size_x, size_y = q_ref.shape[1], q_ref.shape[2]
    q_flat = q_ref.reshape(5, size_x * size_y, LANES)
    ty_flat = ty_ref.reshape(5, size_y * size_x, LANES)
    shock = mask_ref[...] > 0.0

    def cells(start, count, load, carry, normal):
        def body(i, before):
            q = load(i)
            half_vel, half_enth, pressure, total, sound = cell_values(q[0], q[1:4], q[4])
            flux = half_flux(q[1:4], half_vel, pressure, total, normal)
            wave = jnp.abs(2.0 * half_vel[normal]) + sound
            half = [0.5 * v for v in q]
            vel = [half_vel[n] for n in pair_order(normal)] + [half_enth]
            now = flux + half + vel + [wave]
            at = start + i
            for c in range(10):
                p_ref[at, c] = now[c] - before[c]
            for c in range(5):
                p_ref[at, 10 + c] = now[c] + before[c]
            for c in range(4):
                p_ref[at, 15 + c] = now[10 + c] + before[10 + c]
            p_ref[at, 19] = jnp.maximum(now[14], before[14])
            return tuple(now)

        return lax.fori_loop(0, count, body, carry)

    def faces(normal, store, with_weno):
        def body(j, before):
            d_flux = [[p_ref[j - 2 + k, c] for c in range(5)] for k in range(5)]
            rest = central_rest(d_flux)
            now = [p_ref[j, 10 + c] + rest[c] for c in range(5)]
            if with_weno:
                d_state = [[p_ref[j - 2 + k, 5 + c] for c in range(5)] for k in range(5)]
                mean = [p_ref[j, 15 + n] for n in range(4)]
                alpha = jnp.maximum(jnp.maximum(p_ref[j - 2, 19], p_ref[j, 19]), p_ref[j + 2, 19])
                weno = weno_rest(d_flux, d_state, mean, alpha, normal)
                now = now + [weno[c] - rest[c] for c in range(5)]
            at = jnp.maximum(j - 4, 0)
            for c in range(5):
                diff = before[c] - now[c]
                if with_weno:
                    diff = diff + jnp.where(shock, before[5 + c] - now[5 + c], 0.0)
                store(at, c, diff)
            return tuple(now)

        zero = jnp.zeros((ROWS, LANES), jnp.float32)
        count = 10 if with_weno else 5
        lax.fori_loop(3, 4 + size_x, body, (zero,) * count)

    def line(normal, left, middle, right, store):
        zero = jnp.zeros((ROWS, LANES), jnp.float32)
        carry = (zero,) * 15
        carry = cells(0, 3, left, carry, normal)
        carry = cells(3, size_x, middle, carry, normal)
        cells(3 + size_x, 3, right, carry, normal)

        @pl.when(any_ref[4 + group] > 0)
        def _():
            faces(normal, store, True)

        @pl.when(any_ref[4 + group] <= 0)
        def _():
            faces(normal, store, False)

    def line_x(t, carry):
        rows = pl.ds(pl.multiple_of(t * ROWS, ROWS), ROWS)

        def store(at, c, diff):
            ten_ref[c, at, rows, :] = az_ref[c, at, rows, :] + diff

        line(
            0,
            lambda i: [xl_ref[c, i, rows, :] for c in range(5)],
            lambda i: [q_ref[c, i, rows, :] for c in range(5)],
            lambda i: [xr_ref[c, i, rows, :] for c in range(5)],
            store,
        )
        return carry

    def line_y(t, carry):
        rows = pl.ds(pl.multiple_of(t * ROWS, ROWS), ROWS)

        def store(at, c, diff):
            ty_ref[c, at, rows, :] = diff

        line(
            1,
            lambda i: [yl_ref[c, i, rows, :] for c in range(5)],
            lambda i: [q_flat[c, pl.ds(t * (ROWS * size_y) + i, ROWS, stride=size_y), :] for c in range(5)],
            lambda i: [yr_ref[c, i, rows, :] for c in range(5)],
            store,
        )
        return carry

    lax.fori_loop(0, size_y // ROWS, line_x, 0)
    lax.fori_loop(0, size_x // ROWS, line_y, 0)
    step = step_ref[0]

    def last(x, carry):
        for t in range(size_y // ROWS):
            rows = pl.ds(t * ROWS, ROWS)
            for c in range(5):
                other = ty_flat[c, pl.ds(t * (ROWS * size_x) + x, ROWS, stride=size_x), :]
                total = ten_ref[c, x, rows, :] + other
                ten_ref[c, x, rows, :] = total
                adv_ref[c, x, rows, :] = q_ref[c, x, rows, :] + step * total
        return carry

    lax.fori_loop(0, size_x, last, 0)


def call_lanes(needs, conserved, mask):
    _, size_x, size_y, size_z = conserved.shape
    groups = size_z // LANES
    tile = (ROWS, LANES)
    return pl.pallas_call(
        along_lanes,
        out_shape=jax.ShapeDtypeStruct(conserved.shape, jnp.float32),
        grid=(size_x,),
        in_specs=[
            pl.BlockSpec(memory_space=pltpu.SMEM),
            pl.BlockSpec((5, 1, size_y, size_z), lambda x: (0, x, 0, 0)),
            pl.BlockSpec((1, size_z), lambda x: (0, 0)),
        ],
        out_specs=pl.BlockSpec((5, 1, size_y, size_z), lambda x: (0, x, 0, 0)),
        scratch_shapes=[
            pltpu.VMEM((groups, 5, 10) + tile, jnp.float32),
            pltpu.VMEM((groups, 5) + tile, jnp.float32),
            pltpu.VMEM((groups, 5) + tile, jnp.float32),
            pltpu.VMEM((groups, 5) + tile, jnp.float32),
            pltpu.VMEM((groups, 5) + tile, jnp.float32),
        ],
        cost_estimate=pl.CostEstimate(flops=120_000_000, bytes_accessed=2 * conserved.size * 4, transcendentals=0),
        name="along_lanes",
    )(needs, conserved, mask)


def call_others(needs, step, conserved, x_low, x_high, y_low, y_high, part, mask):
    _, size_x, size_y, size_z = conserved.shape
    groups = size_z // LANES
    tile = (ROWS, LANES)

    def spec(first, second):
        return pl.BlockSpec((5, first, second, LANES), lambda g: (0, 0, 0, g))

    smem = pl.BlockSpec(memory_space=pltpu.SMEM)
    whole = spec(size_x, size_y)
    return pl.pallas_call(
        along_others,
        out_shape=[jax.ShapeDtypeStruct(conserved.shape, jnp.float32)] * 2,
        grid=(groups,),
        in_specs=[
            smem,
            smem,
            whole,
            spec(3, size_y),
            spec(3, size_y),
            spec(3, size_x),
            spec(3, size_x),
            whole,
            pl.BlockSpec((1, LANES), lambda g: (0, g)),
        ],
        out_specs=[whole, whole],
        scratch_shapes=[
            pltpu.VMEM((size_x + 6, 20) + tile, jnp.float32),
            pltpu.VMEM((5, size_y, size_x, LANES), jnp.float32),
        ],
        cost_estimate=pl.CostEstimate(flops=240_000_000, bytes_accessed=4 * conserved.size * 4, transcendentals=0),
        name="along_others",
    )(needs, step, conserved, x_low, x_high, y_low, y_high, part, mask)


def speed_max(fields):
    density = fields[0]
    kinetic = 0.5 * (fields[1] * fields[1] + fields[2] * fields[2] + fields[3] * fields[3])
    pressure = GAMMA_LESS * (fields[4] - kinetic / density)
    sound_speed = jnp.sqrt(GAMMA * pressure / density)
    total = jnp.abs(fields[1]) + jnp.abs(fields[2]) + jnp.abs(fields[3])
    return jnp.max(total / density + 3.0 * sound_speed)


def needs_of(flags, groups):
    per = flags.shape[0] // groups
    own = jnp.max(flags.reshape(groups, per), axis=1)
    last = jnp.roll(flags.reshape(groups, per)[:, -1], 1)
    return jnp.concatenate([jnp.maximum(own, last), own])


def pieces(axis, shard, dim):
    size = lax.axis_size(axis)
    length = shard.shape[dim]
    up = [(i, (i + 1) % size) for i in range(size)]
    down = [(j, i) for i, j in up]
    last = lax.slice_in_dim(shard, length - 3, length, axis=dim)
    first = lax.slice_in_dim(shard, 0, 3, axis=dim)
    if dim == 2:
        last, first = (jnp.swapaxes(v, 1, 2) for v in (last, first))
    return lax.ppermute(last, axis, up), lax.ppermute(first, axis, down)


def top_of_all(value):
    count = lax.axis_size("gx") * lax.axis_size("gy")
    rows = jnp.full((count, LANES), value, jnp.float32)
    return jnp.max(lax.all_to_all(rows, ("gx", "gy"), 0, 0, tiled=True))


def shards(conserved, shock_flags):
    size_x, size_z = conserved.shape[1], conserved.shape[3]
    flags = shock_flags[0, 0]
    top = speed_max(conserved)
    x_low, x_high = pieces("gx", conserved, 1)
    y_low, y_high = pieces("gy", conserved, 2)
    step = (COURANT / top_of_all(top)).reshape(1)
    mask = jnp.repeat(flags, size_x).astype(jnp.float32)[None, :]
    needs = needs_of(flags, size_z // LANES)
    part = call_lanes(needs, conserved, mask)
    advanced, tendency = call_others(needs, step, conserved, x_low, x_high, y_low, y_high, part, mask)
    return advanced, tendency


def solution(mesh):
    return jax.shard_map(
        shards,
        mesh=mesh,
        in_specs=(P(None, "gx", "gy", None), P("gx", "gy", None)),
        out_specs=(P(None, "gx", "gy", None), P(None, "gx", "gy", None)),
        check_vma=False,
    )
```

time: 528 us -> 128 us (0.24)
  the two profiles are of different devices: /device:TPU:8 before, /device:TPU:16 now
where the time goes in v1:
time: 128 us; the launch traced here: 129 us
  Pallas kernels  92.1 us (72%)
  starting transfers between devices  23.1 us (18%)
  local copies, waits for them, and re-layouts  6.32 us (5%)
  other arithmetic  5.76 us (4%)
  between operations  1.4 us (1%)
    pallas_call x1, Pallas kernels, call_others(): pl.pallas_call(along_others, out_shape=[jax.ShapeDtypeStruct(conserved.sh...  53.3 us
    pallas_call x1, Pallas kernels, call_lanes(): pl.pallas_call(along_lanes, out_shape=jax.ShapeDtypeStruct(conserved.shap...  38.8 us
    all_to_all x1, starting transfers between devices, top_of_all(): return jnp.max(lax.all_to_all(rows, ('gx', 'gy'), 0, 0, tiled=True))  14.5 us
    ppermute x4, starting transfers between devices, pieces(): return (lax.ppermute(last, axis, up), lax.ppermute(first, axis, down))  8.64 us
    reduce_max x1, other arithmetic, speed_max(): return jnp.max(total / density + 3.0 * sound_speed)  2.89 us
  transfers between devices with their start and end apart: 5, of which 0 were waited for; matrix products, arithmetic and copies ran while one was open for 5% of the time, Pallas kernels for 30%

profile of v1, /device:TPU:16, one launch (start us, length us, event | category | flops | bytes accessed | tf_op | source)
XLA Modules:
  0.0 128.7 jit_solution(11718153478794967767)
XLA Ops:
  0.6 0.0 copy-start
  0.6 2.9 %fusion.4 = f32[]{:T(128)} fusion(f32[5,16,16,512]{3,2,1,0:T(8,128)} %q_ref.3), kind=kLoop, calls=%fused_computation.6 | loop fusion | flops 2490367 | bytes 2621444 | tf_op jit(solution)/shard_map/reduce_max | solution.py:382
  3.5 1.4 %broadcast_in_dim.7 = f32[256,1,128]{2,1,0:T(1,128)} broadcast(f32[]{:T(128)} %fusion.4), dimensions={} | broadcast | bytes 131076 | tf_op jit(solution)/shard_map/broadcast_in_dim | solution.py:406
  4.9 14.5 %all-to-all-start = ((f32[256,1,128]{2,1,0:T(1,128)}), f32[256,1,128]{2,1,0:T(1,128)S(1)}, u32[]{:S(2)}, u32[]{:S(2)}) async-start(f32[256,1,128]{2,1,0:T(1,128)} %broadcast_in_dim.7), calls=%async_computation | async-start | bytes 262144 | tf_op jit(solution)/shard_map/all_to_all | solution.py:407
  19.4 1.0 fusion.6
  20.4 6.5 %collective-permute-start.1 = (f32[5,3,16,512]{3,2,1,0:T(8,128)}, f32[5,3,16,512]{3,2,1,0:T(8,128)S(1)}, u32[]{:S(2)}, u32[]{:S(2)}) collective-permute-start(f32[5,3,16,512]{3,2,1,0:T(8,128)} %get-tuple-element.4), channel_id=1, source_target_pairs={{4,0},{8,4},{12,8},{16,12},{20,16},{24,20},{28,24},{32,28},{36,32}... | collective-permute-start | bytes 1474568 | tf_op jit(solution)/shard_map/ppermute | solution.py:401
  26.9 0.0 collective-permute-start
  26.9 0.3 fusion.5
  27.2 0.2 copy.18
  27.4 1.3 %collective-permute-start.2 = (f32[5,3,16,512]{3,2,1,0:T(8,128)S(1)}, f32[5,3,16,512]{3,2,1,0:T(8,128)S(1)}, u32[]{:S(2)}, u32[]{:S(2)}) collective-permute-start(f32[5,3,16,512]{3,2,1,0:T(8,128)S(1)} %bitcast.43), channel_id=1, source_target_pairs={{0,1},{1,2},{2,3},{3,0},{4,5},{5,6},{6,7},{7,4},{8,9},{9,10},{10,1... | collective-permute-start | bytes 1474568 | tf_op jit(solution)/shard_map/ppermute | solution.py:401
  28.7 0.2 copy.17
  28.8 0.9 collective-permute-start.3
  29.7 0.6 broadcast.9
  30.3 0.7 convert_bitcast_fusion
  31.0 0.1 reshape_squeeze.4
  31.1 0.7 slice.50
  31.7 0.1 reduce_max.27
  31.9 0.1 broadcast_in_dim.8
  31.9 0.7 convert_element_type.19.mask_ref
  32.6 0.2 slice_reduce_fusion
  32.8 0.8 add_maximum_fusion
  33.5 0.7 pad_add_fusion.any_ref
  34.2 38.8 %along_lanes.1.az_ref = f32[5,16,16,512]{3,2,1,0:T(8,128)} custom-call(s32[8]{0:T(128)} %pad_add_fusion.any_ref, f32[5,16,16,512]{3,2,1,0:T(8,128)} %q_ref.3, f32[1,512]{1,0:T(1,128)} %convert_element_type.19.mask_ref), custom_call_target="tpu_custom_call" | custom-call | flops 120000000 | bytes 5242880 | tf_op jit(solution)/shard_map/along_lanes/pallas_call | solution.py:319
  73.0 0.0 all-to-all-done
  73.0 0.6 reduce_max.29
  74.3 0.0 collective-permute-done.1.xr_ref
  74.3 0.0 collective-permute-done.2.yl_ref
  74.3 0.0 collective-permute-done.3.yr_ref
  74.4 0.7 copy-done.1
  75.1 0.2 copy-done.2
  75.3 0.2 copy-done.3
  75.4 53.3 %along_others.1 = (f32[5,16,16,512]{3,2,1,0:T(8,128)}, f32[5,16,16,512]{3,2,1,0:T(8,128)}) custom-call(s32[8]{0:T(128)} %pad_add_fusion.any_ref, f32[1]{0:T(128)} %bitcast.6.step_ref, f32[5,16,16,512]{3,2,1,0:T(8,128)} %q_ref.3, f32[5,3,16,512]{3,2,1,0:T(8,128)} %collective-permute-done.xl_ref, f32[5,3,16,512]{3,2,1,0:T(8,128)} %copy-done.1, ...), custom_call_target="tpu_custom_call" | custom-call | flops 240000000 | bytes 10485760 | tf_op jit(solution)/shard_map/along_others/pallas_call | solution.py:351
  (7 shorter events, 0.0 us)
Async XLA Ops:
  0.6 18.8 %copy-start = (f32[5,16,16,512]{3,2,1,0:T(8,128)S(1)}, f32[5,16,16,512]{3,2,1,0:T(8,128)}, u32[]{:S(2)}) copy-start(f32[5,16,16,512]{3,2,1,0:T(8,128)} %q_ref.3) | copy-start | bytes 7864324
  4.9 68.1 %all-to-all-start = ((f32[256,1,128]{2,1,0:T(1,128)}), f32[256,1,128]{2,1,0:T(1,128)S(1)}, u32[]{:S(2)}, u32[]{:S(2)}) async-start(f32[256,1,128]{2,1,0:T(1,128)} %broadcast_in_dim.7), calls=%async_computation | async-start | bytes 262144 | tf_op jit(solution)/shard_map/all_to_all | solution.py:407
  20.4 9.9 %copy-start.4 = (s32[1,1,32]{2,1,0:T(1,128)S(1)}, s32[1,1,32]{2,1,0:T(1,128)}, u32[]{:S(2)}) copy-start(s32[1,1,32]{2,1,0:T(1,128)} %param.3) | copy-start | bytes 388
  20.4 53.9 %collective-permute-start.1 = (f32[5,3,16,512]{3,2,1,0:T(8,128)}, f32[5,3,16,512]{3,2,1,0:T(8,128)S(1)}, u32[]{:S(2)}, u32[]{:S(2)}) collective-permute-start(f32[5,3,16,512]{3,2,1,0:T(8,128)} %get-tuple-element.4), channel_id=1, source_target_pairs={{4,0},{8,4},{12,8},{16,12},{20,16},{24,20},{28,24},{32,28},{36,32}... | collective-permute-start | bytes 1474568 | tf_op jit(solution)/shard_map/ppermute | solution.py:401
  26.9 47.4 %collective-permute-start = (f32[5,3,16,512]{3,2,1,0:T(8,128)}, f32[5,3,16,512]{3,2,1,0:T(8,128)}, u32[]{:S(2)}, u32[]{:S(2)}) collective-permute-start(f32[5,3,16,512]{3,2,1,0:T(8,128)} %get-tuple-element.5), channel_id=1, source_target_pairs={{0,4},{4,8},{8,12},{12,16},{16,20},{20,24},{24,28},{28,32},{32,36}... | collective-permute-start | bytes 1474568 | tf_op jit(solution)/shard_map/ppermute | solution.py:401
  27.4 47.0 %collective-permute-start.2 = (f32[5,3,16,512]{3,2,1,0:T(8,128)S(1)}, f32[5,3,16,512]{3,2,1,0:T(8,128)S(1)}, u32[]{:S(2)}, u32[]{:S(2)}) collective-permute-start(f32[5,3,16,512]{3,2,1,0:T(8,128)S(1)} %bitcast.43), channel_id=1, source_target_pairs={{0,1},{1,2},{2,3},{3,0},{4,5},{5,6},{6,7},{7,4},{8,9},{9,10},{10,1... | collective-permute-start | bytes 1474568 | tf_op jit(solution)/shard_map/ppermute | solution.py:401
  28.8 45.5 %collective-permute-start.3 = (f32[5,3,16,512]{3,2,1,0:T(8,128)S(1)}, f32[5,3,16,512]{3,2,1,0:T(8,128)S(1)}, u32[]{:S(2)}, u32[]{:S(2)}) collective-permute-start(f32[5,3,16,512]{3,2,1,0:T(8,128)S(1)} %bitcast.44), channel_id=1, source_target_pairs={{1,0},{2,1},{3,2},{0,3},{5,4},{6,5},{7,6},{4,7},{9,8},{10,9},{11,1... | collective-permute-start | bytes 1474568 | tf_op jit(solution)/shard_map/ppermute | solution.py:401
  74.3 0.8 copy-start.1
  74.3 0.9 copy-start.2
  74.3 1.1 copy-start.3

commit v2 on v1

v2 whole, which is shorter than its diff:
```python
import functools

import jax
import jax.numpy as jnp
from jax import lax
from jax.experimental import pallas as pl
from jax.experimental.pallas import tpu as pltpu
from jax.sharding import PartitionSpec as P

GAMMA = 1.4
GAMMA_LESS = 0.4
COURANT = 0.4
EPSILON = 1e-06
LANES = 128
ROWS = 8
TINY = 1e-37


def cell_values(density, mom, energy, normal):
    inv = 1.0 / density
    inv_half = 0.5 * inv
    half_vel = [m * inv_half for m in mom]
    kinetic = mom[0] * half_vel[0] + mom[1] * half_vel[1] + mom[2] * half_vel[2]
    pressure = GAMMA_LESS * (energy - kinetic)
    total = energy + pressure
    sound_sq = GAMMA * pressure * inv
    sound = sound_sq * lax.rsqrt(jnp.maximum(sound_sq, TINY))
    half = [0.5 * v for v in (density, *mom, energy)]
    half_normal = half_vel[normal]
    flux = [half[1 + normal]]
    for other in range(3):
        part = mom[other] * half_normal
        flux.append(part + 0.5 * pressure if other == normal else part)
    flux.append(total * half_normal)
    means = [half_vel[n] for n in pair_order(normal)] + [total * inv_half]
    return half, flux, means, jnp.abs(2.0 * half_normal) + sound


def pair_order(normal):
    return [normal] + [other for other in range(3) if other != normal]


def recon_rest(d1, d2, d3, d4):
    t1 = d2 - d1
    t2 = d3 - d2
    t3 = d4 - d3
    d2s = 0.75 * d2
    d3s = 0.75 * d3
    p2 = d2s * d2 + 0.75 * EPSILON
    p3 = d3s * d3 + 0.75 * EPSILON
    r0 = 1.0 / (t1 * (t1 + d2s) + p2)
    r1 = 1.0 / (t2 * (t2 + d2s) + p2)
    r2 = 1.0 / (t3 * (t3 - d3s) + p3)
    z0 = r0 * r0
    z1 = r1 * r1
    z2 = 1.5 * (r2 * r2)
    num = z0 * (t2 - t1) + z2 * (t3 - t2)
    den = z2 + (0.5 * z0 + 3.0 * z1)
    return num * (1.0 / den)


def central_face(sums, d_flux):
    return [
        sums[c] + (1.0 / 30.0) * ((d_flux[4][c] - d_flux[0][c]) - 7.0 * (d_flux[3][c] - d_flux[1][c]))
        for c in range(5)
    ]


def face_terms(means):
    a, b, e, h = means
    k = 0.5 * (a * a + b * b + e * e)
    s_sq = GAMMA_LESS * (h - k)
    inv_s = lax.rsqrt(s_sq)
    return [a, b, e, h, k, s_sq * inv_s, (0.5 * GAMMA_LESS) * (inv_s * inv_s), 0.5 * inv_s]


def face_order(normal):
    return [0] + [1 + n for n in pair_order(normal)] + [4]


def weno_waves(d_flux, d_state, terms, alpha, normal):
    order = face_order(normal)
    a, b, e, _, k, _, half_g, half_inv = terms

    def project(x):
        x1 = x[1] - a * x[0]
        x2 = x[2] - b * x[0]
        x3 = x[3] - e * x[0]
        y = half_g * (x[4] - a * x1 - b * x2 - e * x3 - k * x[0])
        z = half_inv * x1
        return [y - z, x[0] - (y + y), x2, x3, y + z]

    up = []
    down = []
    for step in range(5):
        scaled = [alpha * d_state[step][c] for c in order]
        flux = [d_flux[step][c] for c in order]
        up.append([f + q for f, q in zip(flux, scaled)] if step < 4 else None)
        down.append([f - q for f, q in zip(flux, scaled)] if step > 0 else None)
    linear = [(up[1][c] - down[3][c]) - (up[2][c] - down[2][c]) for c in range(5)]
    up = [project(x) if x is not None else None for x in up]
    down = [project(x) if x is not None else None for x in down]
    waves = [
        recon_rest(up[0][c], up[1][c], up[2][c], up[3][c])
        - recon_rest(down[4][c], down[3][c], down[2][c], down[1][c])
        for c in range(5)
    ]
    return linear, waves


def weno_face(sums, linear, waves, terms, normal):
    a, b, e, h, k, s = terms[:6]
    outer = waves[0] + waves[4]
    shared = outer + waves[1]
    swing = s * (waves[4] - waves[0])
    back = [
        shared,
        a * shared + swing,
        b * shared + waves[2],
        e * shared + waves[3],
        h * outer + k * waves[1] + b * waves[2] + e * waves[3] + a * swing,
    ]
    face = [None] * 5
    for position, component in enumerate(face_order(normal)):
        face[component] = sums[component] + (1.0 / 6.0) * (linear[position] - back[position])
    return face


class Line:
    def __init__(self, refs, normal, unit):
        self.v_ref, self.p_ref, self.w_ref, self.f_ref = refs
        self.normal = normal
        self.unit = unit

    def rows(self, i, off=0):
        start = i * ROWS + off * self.unit
        if (off * self.unit) % ROWS == 0 and not isinstance(i, int):
            start = pl.multiple_of(start, ROWS)
        return pl.ds(start, ROWS)

    def cell(self, i, q):
        n = self.normal
        half, flux, means, wave = cell_values(q[0], q[1:4], q[4], n)
        now = half + flux[1:] + means + [wave]
        here, prev = self.rows(i), self.rows(i, -1)
        for v in range(14):
            self.v_ref[v, here, :] = now[v]
        before = [self.v_ref[v, prev, :] for v in range(14)]
        for v in range(9):
            self.p_ref[v, here, :] = now[v] - before[v]
        self.p_ref[9, here, :] = now[1 + n] + before[1 + n]
        for v in range(5, 9):
            self.p_ref[5 + v, here, :] = now[v] + before[v]
        self.p_ref[14, here, :] = jnp.maximum(now[13], before[13])
        terms = face_terms([now[v] + before[v] for v in range(9, 13)])
        for v in range(8):
            self.p_ref[15 + v, here, :] = terms[v]

    def pair(self, v, j, off=0):
        return self.p_ref[v, self.rows(j, off), :]

    def fluxes(self, j):
        return [[self.pair(4 + c if c else 1 + self.normal, j, k - 2) for c in range(5)] for k in range(5)]

    def central(self, j, d_flux):
        face = central_face([self.pair(9 + c, j) for c in range(5)], d_flux)
        for c in range(5):
            self.f_ref[c, self.rows(j), :] = face[c]

    def waves(self, j, d_flux):
        d_state = [[self.pair(c, j, k - 2) for c in range(5)] for k in range(5)]
        terms = [self.pair(15 + v, j) for v in range(8)]
        alpha = jnp.maximum(jnp.maximum(self.pair(14, j, -2), self.pair(14, j)), self.pair(14, j, 2))
        linear, waves = weno_waves(d_flux, d_state, terms, alpha, self.normal)
        for c in range(5):
            self.w_ref[c, self.rows(j), :] = linear[c]
            self.w_ref[5 + c, self.rows(j), :] = waves[c]

    def face(self, j):
        both = [self.w_ref[c, self.rows(j), :] for c in range(10)]
        terms = [self.pair(15 + v, j) for v in range(6)]
        face = weno_face([self.pair(9 + c, j) for c in range(5)], both[:5], both[5:], terms, self.normal)
        for c in range(5):
            self.f_ref[5 + c, self.rows(j), :] = face[c]

    def change(self, j, first):
        here, following = self.rows(j), self.rows(j, 1)
        return [self.f_ref[first + c, here, :] - self.f_ref[first + c, following, :] for c in range(5)]


def along_lanes(flag_ref, q_ref, out_ref, z_ref, v_ref, p_ref, w_ref, f_ref):
    size_x, size_y, width = q_ref.shape[1:]
    lines = size_x * size_y
    q_flat = q_ref.reshape(5, lines, width)
    out_flat = out_ref.reshape(5, lines, width)
    groups = width // LANES
    steps = width // ROWS
    blocks = flag_ref.shape[2]
    per_block = steps // blocks
    line = Line((v_ref, p_ref, w_ref, f_ref), 2, 1)

    def turn_in(g, carry):
        lanes = pl.ds(pl.multiple_of(g * LANES, LANES), LANES)
        for c in range(5):
            z_ref[c, lanes, :] = q_flat[c, :, lanes].T
        return carry

    def turn_out(g, carry):
        lanes = pl.ds(pl.multiple_of(g * LANES, LANES), LANES)
        for c in range(5):
            out_flat[c, :, lanes] = z_ref[5 + c, lanes, :].T
        return carry

    def chunk_of(i):
        return lax.rem(jnp.int32(i + (steps - 2)), steps)

    def fetch(i):
        at = chunk_of(i)
        rows = pl.ds(pl.multiple_of(at * ROWS, ROWS), ROWS)
        return [z_ref[c, rows, :] for c in range(5)]

    def block_of(i):
        return chunk_of(i) // per_block

    def finish(j):
        at = jnp.maximum(j - 2, 0)
        rows = pl.ds(pl.multiple_of(at * ROWS, ROWS), ROWS)
        first = jnp.where(flag_ref[0, 0, block_of(j)] > 0, 5, 0)
        for c, value in enumerate(line.change(j, first)):
            z_ref[5 + c, rows, :] = value

    lax.fori_loop(0, groups, turn_in, 0)

    def lead(i, carry):
        line.cell(i, fetch(i))
        return carry

    lax.fori_loop(1, 4, lead, 0)

    def needed(i):
        return flag_ref[0, 0, block_of(i)] + flag_ref[0, 0, block_of(i - 1)]

    def body(i, carry):
        sharp = needed(i) + needed(i - 1)

        @pl.when(sharp > 0)
        def _():
            line.face(i - 1)
            finish(i - 2)
            d_flux = line.fluxes(i)
            line.waves(i, d_flux)
            line.central(i, d_flux)
            line.cell(i + 2, fetch(i + 2))

        @pl.when(sharp <= 0)
        def _():
            finish(i - 2)
            line.central(i, line.fluxes(i))
            line.cell(i + 2, fetch(i + 2))

        return carry

    lax.fori_loop(2, steps + 2, body, 0)
    line.face(steps + 1)
    for c in range(10):
        f_ref[c, pl.ds(ROWS * (steps + 2), ROWS), :] = f_ref[c, pl.ds(2 * ROWS, ROWS), :]
    finish(steps)
    finish(steps + 1)
    lax.fori_loop(0, groups, turn_out, 0)


def along_others(
    flag_ref, top_ref, q_ref, xl_ref, xr_ref, yl_ref, yr_ref, za_ref, zb_ref, adv_ref, ten_ref, v_ref, p_ref, w_ref, f_ref, ty_ref
):
    group = pl.program_id(0)
    size_x, size_y = q_ref.shape[1], q_ref.shape[2]
    q_flat = q_ref.reshape(5, size_x * size_y, LANES)
    ty_flat = ty_ref.reshape(5, size_y * size_x, LANES)
    per_group = flag_ref.shape[2] // pl.num_programs(0)
    edge = LANES // per_group
    lane_block = lax.broadcasted_iota(jnp.int32, (ROWS, LANES), 1) // edge
    marks = jnp.zeros((ROWS, LANES), jnp.int32)
    some = jnp.int32(0)
    for b in range(per_group):
        flag = flag_ref[0, 0, group * per_group + b]
        marks = jnp.where(lane_block == b, flag, marks)
        some = jnp.maximum(some, flag)
    shock = marks > 0

    def march(normal, count, left, middle, right, store):
        line = Line((v_ref, p_ref, w_ref, f_ref), normal, ROWS)

        def from_left(i, carry):
            line.cell(1 + i, left(i))
            return carry

        def from_middle(i, carry):
            line.cell(4 + i, middle(i))
            return carry

        lax.fori_loop(0, 3, from_left, 0)
        lax.fori_loop(0, 3, from_middle, 0)

        def ahead(j):
            inner = j - 1 < count
            near = middle(jnp.minimum(j - 1, count - 1))
            far = right(jnp.clip(j - 1 - count, 0, 2))
            line.cell(j + 3, [jnp.where(inner, n, f) for n, f in zip(near, far)])

        def finish(j, sharp):
            at = jnp.maximum(j - 4, 0)
            change = line.change(j, 0)
            if sharp:
                change = [jnp.where(shock, w, c) for w, c in zip(line.change(j, 5), change)]
            for c in range(5):
                store(at, c, change[c])

        @pl.when(some > 0)
        def _():
            def body(j, carry):
                line.face(j - 1)
                finish(j - 2, True)
                d_flux = line.fluxes(j)
                line.waves(j, d_flux)
                line.central(j, d_flux)
                ahead(j)
                return carry

            lax.fori_loop(4, 5 + count, body, 0)
            line.face(4 + count)
            finish(3 + count, True)

        @pl.when(some <= 0)
        def _():
            def body(j, carry):
                ahead(j)
                line.central(j, line.fluxes(j))
                finish(j - 1, False)
                return carry

            lax.fori_loop(4, 5 + count, body, 0)

    def line_x(t, carry):
        rows = pl.ds(pl.multiple_of(t * ROWS, ROWS), ROWS)

        def store(at, c, value):
            ten_ref[c, at, rows, :] = value

        march(
            0,
            size_x,
            lambda i: [xl_ref[c, i, rows, :] for c in range(5)],
            lambda i: [q_ref[c, i, rows, :] for c in range(5)],
            lambda i: [xr_ref[c, i, rows, :] for c in range(5)],
            store,
        )
        return carry

    def line_y(t, carry):
        rows = pl.ds(pl.multiple_of(t * ROWS, ROWS), ROWS)

        def store(at, c, value):
            ty_ref[c, at, rows, :] = value

        march(
            1,
            size_y,
            lambda i: [yl_ref[c, i, rows, :] for c in range(5)],
            lambda i: [q_flat[c, pl.ds(t * (ROWS * size_y) + i, ROWS, stride=size_y), :] for c in range(5)],
            lambda i: [yr_ref[c, i, rows, :] for c in range(5)],
            store,
        )
        return carry

    lax.fori_loop(0, size_y // ROWS, line_x, 0)
    lax.fori_loop(0, size_x // ROWS, line_y, 0)
    step = COURANT / jnp.max(top_ref[...], axis=0, keepdims=True)
    half = size_x // 2

    def last(x, carry):
        for h, part_ref in enumerate((za_ref, zb_ref)):
            for t in range(size_y // ROWS):
                rows = pl.ds(t * ROWS, ROWS)
                for c in range(5):
                    at = h * half + x
                    other = ty_flat[c, pl.ds(t * (ROWS * size_x) + at, ROWS, stride=size_x), :]
                    total = ten_ref[c, at, rows, :] + other + part_ref[c, x, rows, :]
                    ten_ref[c, at, rows, :] = total
                    adv_ref[c, at, rows, :] = q_ref[c, at, rows, :] + step * total
        return carry

    lax.fori_loop(0, half, last, 0)


def prepare(q_ref, xf_ref, xl_ref, yf_ref, yl_ref, top_ref, acc_ref):
    size_x, size_y = q_ref.shape[1], q_ref.shape[2]
    q_flat = q_ref.reshape(5, size_x * size_y, LANES)
    group = pl.program_id(0)

    @pl.when(group == 0)
    def _():
        acc_ref[...] = jnp.zeros_like(acc_ref)

    def speeds(x, top):
        for t in range(size_y // ROWS):
            q = [q_ref[c, x, pl.ds(t * ROWS, ROWS), :] for c in range(5)]
            inv = 1.0 / q[0]
            kinetic = 0.5 * (q[1] * q[1] + q[2] * q[2] + q[3] * q[3]) * inv
            sound_sq = (GAMMA * GAMMA_LESS) * (q[4] - kinetic) * inv
            sound = sound_sq * lax.rsqrt(jnp.maximum(sound_sq, TINY))
            total = (jnp.abs(q[1]) + jnp.abs(q[2]) + jnp.abs(q[3])) * inv + 3.0 * sound
            top = jnp.maximum(top, total)
        return top

    acc_ref[...] = lax.fori_loop(0, size_x, speeds, acc_ref[...])
    for c in range(5):
        for k in range(3):
            xf_ref[c, k] = q_ref[c, k]
            xl_ref[c, k] = q_ref[c, size_x - 3 + k]
            for t in range(size_x // ROWS):
                rows = pl.ds(t * ROWS, ROWS)
                first = t * ROWS * size_y
                yf_ref[c, k, rows, :] = q_flat[c, pl.ds(first + k, ROWS, stride=size_y), :]
                yl_ref[c, k, rows, :] = q_flat[c, pl.ds(first + size_y - 3 + k, ROWS, stride=size_y), :]

    @pl.when(group == pl.num_programs(0) - 1)
    def _():
        top_ref[...] = jnp.full(top_ref.shape, jnp.max(acc_ref[...]), jnp.float32)


def line_scratch(rows):
    return [pltpu.VMEM((count, rows, LANES), jnp.float32) for count in (14, 23, 10, 10)]


def call_prepare(conserved, rows):
    _, size_x, size_y, size_z = conserved.shape

    def spec(first, second):
        return pl.BlockSpec((5, first, second, LANES), lambda g: (0, 0, 0, g))

    layers = jax.ShapeDtypeStruct((5, 3, size_y, size_z), jnp.float32)
    turned = jax.ShapeDtypeStruct((5, 3, size_x, size_z), jnp.float32)
    return pl.pallas_call(
        prepare,
        out_shape=[layers, layers, turned, turned, jax.ShapeDtypeStruct((rows, LANES), jnp.float32)],
        grid=(size_z // LANES,),
        in_specs=[spec(size_x, size_y)],
        out_specs=[spec(3, size_y), spec(3, size_y), spec(3, size_x), spec(3, size_x)]
        + [pl.BlockSpec((rows, LANES), lambda g: (0, 0))],
        scratch_shapes=[pltpu.VMEM((ROWS, LANES), jnp.float32)],
        cost_estimate=pl.CostEstimate(flops=4_000_000, bytes_accessed=2 * conserved.size * 4, transcendentals=0),
        name="prepare",
    )(conserved)


def call_lanes(flags, conserved, part):
    _, size_x, size_y, size_z = conserved.shape
    chunk = LANES // size_y
    block = (5, chunk, size_y, size_z)
    return pl.pallas_call(
        along_lanes,
        out_shape=jax.ShapeDtypeStruct(block, jnp.float32),
        grid=(1,),
        in_specs=[pl.BlockSpec(memory_space=pltpu.SMEM), pl.BlockSpec(block, lambda _: (0, part, 0, 0))],
        out_specs=pl.BlockSpec(block, lambda _: (0, 0, 0, 0)),
        scratch_shapes=[pltpu.VMEM((10, size_z, LANES), jnp.float32)] + line_scratch(size_z + 5 * ROWS),
        cost_estimate=pl.CostEstimate(flops=60_000_000, bytes_accessed=conserved.size * 4, transcendentals=0),
        name="along_lanes",
    )(flags, conserved)


def call_others(flags, top, conserved, x_low, x_high, y_low, y_high, parts):
    _, size_x, size_y, size_z = conserved.shape

    def spec(first, second):
        return pl.BlockSpec((5, first, second, LANES), lambda g: (0, 0, 0, g))

    whole = spec(size_x, size_y)
    return pl.pallas_call(
        along_others,
        out_shape=[jax.ShapeDtypeStruct(conserved.shape, jnp.float32)] * 2,
        grid=(size_z // LANES,),
        in_specs=[
            pl.BlockSpec(memory_space=pltpu.SMEM),
            pl.BlockSpec(top.shape, lambda g: (0, 0)),
            whole,
            spec(3, size_y),
            spec(3, size_y),
            spec(3, size_x),
            spec(3, size_x),
            spec(size_x // 2, size_y),
            spec(size_x // 2, size_y),
        ],
        out_specs=[whole, whole],
        scratch_shapes=line_scratch((max(size_x, size_y) + 9) * ROWS)
        + [pltpu.VMEM((5, size_y, size_x, LANES), jnp.float32)],
        cost_estimate=pl.CostEstimate(flops=240_000_000, bytes_accessed=4 * conserved.size * 4, transcendentals=0),
        name="along_others",
    )(flags, top, conserved, x_low, x_high, y_low, y_high, *parts)


GX = ("ga", "gb")
SPLIT = 4


def neighbours(axis, first, last):
    size = lax.axis_size(axis)
    up = [(i, (i + 1) % size) for i in range(size)]
    down = [(j, i) for i, j in up]
    return lax.ppermute(last, axis, up), lax.ppermute(first, axis, down)


def swap(rows, axes):
    return lax.all_to_all(rows, axes, 0, 0, tiled=True)


def shards(conserved, shock_flags):
    inner, outer = ("gb",), ("ga", "gy")
    count, others = lax.axis_size(inner), lax.axis_size(outer)
    x_first, x_last, y_first, y_last, top = call_prepare(conserved, count)
    x_low, x_high = neighbours(GX, x_first, x_last)
    y_low, y_high = neighbours("gy", y_first, y_last)
    top = swap(top, inner)
    parts = [call_lanes(shock_flags, conserved, 0)]
    top, parts[0] = lax.optimization_barrier((top, parts[0]))
    top = swap(jnp.broadcast_to(jnp.max(top, axis=0, keepdims=True), (others, LANES)), outer)
    parts.append(call_lanes(shock_flags, conserved, 1))
    return call_others(shock_flags, top, conserved, x_low, x_high, y_low, y_high, parts)


def local(conserved, shock_flags, top, x_low, x_high, y_low, y_high):
    x_first, x_last, y_first, y_last, mine = call_prepare(conserved, 16)
    parts = [call_lanes(shock_flags, conserved, h) for h in range(2)]
    return call_others(shock_flags, mine, conserved, x_last, x_first, y_last, y_first, parts)


def solution(mesh):
    devices = mesh.devices
    size_x, size_y = devices.shape
    mesh = jax.sharding.Mesh(devices.reshape(SPLIT, size_x // SPLIT, size_y), (*GX, "gy"))
    spec = P(None, GX, "gy", None)
    return jax.shard_map(
        shards,
        mesh=mesh,
        in_specs=(spec, P(GX, "gy", None)),
        out_specs=(spec, spec),
        check_vma=False,
    )
```

time: 128 us -> 98.7 us (0.77)
  the two profiles are of different devices: /device:TPU:16 before, /device:TPU:60 now
where the time goes in v2:
time: 98.7 us; the launch traced here: 98.2 us
  Pallas kernels  75.2 us (76%)
  starting transfers between devices  20.4 us (21%)
  local copies, waits for them, and re-layouts  1.82 us (2%)
    pallas_call x1, Pallas kernels, call_others(): pl.pallas_call(along_others, out_shape=[jax.ShapeDtypeStruct(conserved.sh...  42.9 us
    pallas_call x2, Pallas kernels, call_lanes(): pl.pallas_call(along_lanes, out_shape=jax.ShapeDtypeStruct(block, jnp.flo...  27.5 us
    all_to_all x2, starting transfers between devices, swap(): return lax.all_to_all(rows, axes, 0, 0, tiled=True)  16.6 us
    pallas_call x1, Pallas kernels, call_prepare(): pl.pallas_call(prepare, out_shape=[layers, layers, turned, turned, jax.Sh...  4.84 us
    ppermute x4, starting transfers between devices, neighbours(): return (lax.ppermute(last, axis, up), lax.ppermute(first, axis, down))  3.82 us
  transfers between devices with their start and end apart: 6, of which 0 were waited for; matrix products, arithmetic and copies ran while one was open for 1% of the time, Pallas kernels for 28%

profile of v2, /device:TPU:60, one launch (start us, length us, event | category | flops | bytes accessed | tf_op | source)
XLA Modules:
  0.0 98.2 jit_solution(17229749887578799736)
XLA Ops:
  0.6 4.8 %prepare.1 = (f32[5,3,16,512]{3,2,1,0:T(8,128)}, f32[5,3,16,512]{3,2,1,0:T(8,128)}, f32[5,3,16,512]{3,2,1,0:T(8,128)}, f32[5,3,16,512]{3,2,1,0:T(8,128)}, f32[16,128]{1,0:T(8,128)}) custom-call(f32[5,16,16,512]{3,2,1,0:T(8,128)} %q_ref.7), custom_call_target="tpu_custom_call" | custom-call | flops 4000000 | bytes 5242880 | tf_op jit(solution)/shard_map/prepare/pallas_call | solution.py:443
  5.5 0.1 collective-permute-start
  5.5 1.7 %collective-permute-start.1 = (f32[5,3,16,512]{3,2,1,0:T(8,128)}, f32[5,3,16,512]{3,2,1,0:T(8,128)S(1)}, u32[]{:S(2)}, u32[]{:S(2)}) collective-permute-start(f32[5,3,16,512]{3,2,1,0:T(8,128)} %get-tuple-element.12), channel_id=1, source_target_pairs={{4,0},{8,4},{12,8},{16,12},{20,16},{24,20},{28,24},{32,28},{36,32}... | collective-permute-start | bytes 1474568 | tf_op jit(solution)/shard_map/ppermute | solution.py:510
  7.3 0.2 collective-permute-start.2
  7.5 1.8 %collective-permute-start.3 = (f32[5,3,16,512]{3,2,1,0:T(8,128)}, f32[5,3,16,512]{3,2,1,0:T(8,128)S(1)}, u32[]{:S(2)}, u32[]{:S(2)}) collective-permute-start(f32[5,3,16,512]{3,2,1,0:T(8,128)} %get-tuple-element.14), channel_id=1, source_target_pairs={{1,0},{2,1},{3,2},{0,3},{5,4},{6,5},{7,6},{4,7},{9,8},{10,9},{11,1... | collective-permute-start | bytes 1474568 | tf_op jit(solution)/shard_map/ppermute | solution.py:510
  9.3 9.2 %all-to-all-start = ((f32[16,1,128]{2,1,0:T(1,128)}), f32[16,1,128]{2,1,0:T(1,128)S(1)}, u32[]{:S(2)}, u32[]{:S(2)}) async-start(f32[16,1,128]{2,1,0:T(1,128)} %bitcast.7), calls=%async_computation | async-start | bytes 16384 | tf_op jit(solution)/shard_map/all_to_all | solution.py:514
  18.5 13.8 %along_lanes.2.za_ref = f32[5,8,16,512]{3,2,1,0:T(8,128)} custom-call(s32[1,1,32]{2,1,0:T(1,128)} %flag_ref.5, f32[5,16,16,512]{3,2,1,0:T(8,128)} %q_ref.7), custom_call_target="tpu_custom_call" | custom-call | flops 60000000 | bytes 2621440 | tf_op jit(solution)/shard_map/along_lanes/pallas_call | solution.py:460
  32.3 0.0 all-to-all-done
  32.3 0.6 broadcast_in_dim.2
  32.9 7.4 %all-to-all-start.1 = ((f32[16,1,128]{2,1,0:T(1,128)}), f32[16,1,128]{2,1,0:T(1,128)S(1)}, u32[]{:S(2)}, u32[]{:S(2)}) async-start(f32[16,1,128]{2,1,0:T(1,128)} %broadcast_in_dim.2), calls=%async_computation.1 | async-start | bytes 16384 | tf_op jit(solution)/shard_map/all_to_all | solution.py:514
  40.3 13.7 %along_lanes.3.zb_ref = f32[5,8,16,512]{3,2,1,0:T(8,128)} custom-call(s32[1,1,32]{2,1,0:T(1,128)} %flag_ref.5, f32[5,16,16,512]{3,2,1,0:T(8,128)} %q_ref.7), custom_call_target="tpu_custom_call" | custom-call | flops 60000000 | bytes 2621440 | tf_op jit(solution)/shard_map/along_lanes/pallas_call | solution.py:460
  54.0 0.0 all-to-all-done.1
  54.0 0.0 copy-start.4
  54.0 0.0 collective-permute-done.xl_ref
  54.0 0.0 copy-start
  54.0 0.0 collective-permute-done.1.xr_ref
  54.0 0.0 copy-start.1
  54.1 0.0 collective-permute-done.2.yl_ref
  54.1 0.0 copy-start.2
  54.1 0.0 collective-permute-done.3.yr_ref
  54.1 0.0 copy-start.3
  54.1 0.5 copy-done.4
  54.6 0.2 copy-done
  54.8 0.2 copy-done.1
  55.0 0.2 copy-done.2
  55.1 0.2 copy-done.3
  55.3 42.9 %along_others.1 = (f32[5,16,16,512]{3,2,1,0:T(8,128)}, f32[5,16,16,512]{3,2,1,0:T(8,128)}) custom-call(s32[1,1,32]{2,1,0:T(1,128)} %flag_ref.5, f32[16,128]{1,0:T(8,128)} %bitcast.6, f32[5,16,16,512]{3,2,1,0:T(8,128)} %q_ref.7, f32[5,3,16,512]{3,2,1,0:T(8,128)} %copy-done, f32[5,3,16,512]{3,2,1,0:T(8,128)} %copy-done.1, f32[5,3,16,512]{3,2,1,0:T(8,128)} %copy-done.2, ...), custom_call_target="tpu_custom_call" | custom-call | flops 240000000 | bytes 10485760 | tf_op jit(solution)/shard_map/along_others/pallas_call | solution.py:479
  (1 shorter events, 0.0 us)
Async XLA Ops:
  5.5 48.6 %collective-permute-start = (f32[5,3,16,512]{3,2,1,0:T(8,128)}, f32[5,3,16,512]{3,2,1,0:T(8,128)S(1)}, u32[]{:S(2)}, u32[]{:S(2)}) collective-permute-start(f32[5,3,16,512]{3,2,1,0:T(8,128)} %get-tuple-element.11), channel_id=1, source_target_pairs={{0,4},{4,8},{8,12},{12,16},{16,20},{20,24},{24,28},{28,32},{32,36}... | collective-permute-start | bytes 1474568 | tf_op jit(solution)/shard_map/ppermute | solution.py:510
  5.5 48.5 %collective-permute-start.1 = (f32[5,3,16,512]{3,2,1,0:T(8,128)}, f32[5,3,16,512]{3,2,1,0:T(8,128)S(1)}, u32[]{:S(2)}, u32[]{:S(2)}) collective-permute-start(f32[5,3,16,512]{3,2,1,0:T(8,128)} %get-tuple-element.12), channel_id=1, source_target_pairs={{4,0},{8,4},{12,8},{16,12},{20,16},{24,20},{28,24},{32,28},{36,32}... | collective-permute-start | bytes 1474568 | tf_op jit(solution)/shard_map/ppermute | solution.py:510
  7.3 46.8 %collective-permute-start.2 = (f32[5,3,16,512]{3,2,1,0:T(8,128)}, f32[5,3,16,512]{3,2,1,0:T(8,128)S(1)}, u32[]{:S(2)}, u32[]{:S(2)}) collective-permute-start(f32[5,3,16,512]{3,2,1,0:T(8,128)} %get-tuple-element.13), channel_id=1, source_target_pairs={{0,1},{1,2},{2,3},{3,0},{4,5},{5,6},{6,7},{7,4},{8,9},{9,10},{10,1... | collective-permute-start | bytes 1474568 | tf_op jit(solution)/shard_map/ppermute | solution.py:510
  7.5 46.6 %collective-permute-start.3 = (f32[5,3,16,512]{3,2,1,0:T(8,128)}, f32[5,3,16,512]{3,2,1,0:T(8,128)S(1)}, u32[]{:S(2)}, u32[]{:S(2)}) collective-permute-start(f32[5,3,16,512]{3,2,1,0:T(8,128)} %get-tuple-element.14), channel_id=1, source_target_pairs={{1,0},{2,1},{3,2},{0,3},{5,4},{6,5},{7,6},{4,7},{9,8},{10,9},{11,1... | collective-permute-start | bytes 1474568 | tf_op jit(solution)/shard_map/ppermute | solution.py:510
  9.3 23.0 %all-to-all-start = ((f32[16,1,128]{2,1,0:T(1,128)}), f32[16,1,128]{2,1,0:T(1,128)S(1)}, u32[]{:S(2)}, u32[]{:S(2)}) async-start(f32[16,1,128]{2,1,0:T(1,128)} %bitcast.7), calls=%async_computation | async-start | bytes 16384 | tf_op jit(solution)/shard_map/all_to_all | solution.py:514
  32.9 21.1 %all-to-all-start.1 = ((f32[16,1,128]{2,1,0:T(1,128)}), f32[16,1,128]{2,1,0:T(1,128)S(1)}, u32[]{:S(2)}, u32[]{:S(2)}) async-start(f32[16,1,128]{2,1,0:T(1,128)} %broadcast_in_dim.2), calls=%async_computation.1 | async-start | bytes 16384 | tf_op jit(solution)/shard_map/all_to_all | solution.py:514
  54.0 0.6 copy-start.4
  54.0 0.8 copy-start
  54.0 0.9 copy-start.1
  54.1 1.1 %copy-start.2 = (f32[5,3,16,512]{3,2,1,0:T(8,128)}, f32[5,3,16,512]{3,2,1,0:T(8,128)S(1)}, u32[]{:S(2)}) copy-start(f32[5,3,16,512]{3,2,1,0:T(8,128)S(1)} %collective-permute-done.2.yl_ref) | copy-start | bytes 1474564
  54.1 1.2 %copy-start.3 = (f32[5,3,16,512]{3,2,1,0:T(8,128)}, f32[5,3,16,512]{3,2,1,0:T(8,128)S(1)}, u32[]{:S(2)}) copy-start(f32[5,3,16,512]{3,2,1,0:T(8,128)S(1)} %collective-permute-done.3.yr_ref) | copy-start | bytes 1474564
